TPU v7x, 32 devices: a whole 2x2x4 slice. The times are simulated.
32 devices in a mesh: dp: 4 (over y, x), row: 4 (over z), col: 2 (over core).
Axes of the slice: x: 2, y: 2, z: 4, core: 2. Of those that a mesh axis runs over, the one named last changes fastest.
Arguments:
- image: bfloat16 [4, 256, 96, 256], P('dp', None, 'row', 'col'), may hold values from -6 to 6
- cotangent: bfloat16 [4, 256, 96, 256], P('dp', None, 'row', 'col'), may hold values from -6 to 6
- w_reduce: bfloat16 [256, 64], replicated, may hold values from -0.375 to 0.375
- w_spatial: bfloat16 [3, 3, 64, 64], replicated, may hold values from -0.25 to 0.25
- w_expand: bfloat16 [64, 256], replicated, may hold values from -0.75 to 0.75
Outputs:
- grad_image: bfloat16 [4, 256, 96, 256], P('dp', None, 'row', 'col')
- grad_reduce: float32 [256, 64], replicated
- grad_spatial: float32 [3, 3, 64, 64], replicated
- grad_expand: float32 [64, 256], replicated
All inputs are finite; a program needn't handle non-finite values.
Results may differ from a plain program's by a relative error of at most 0.0061.
Values may be sent and summed in bfloat16 or wider, within the bound.
A program may use at most 64 MiB of HBM per device.

v0:
```python
import jax
import jax.numpy as jnp
from jax import lax
from jax.sharding import PartitionSpec as P

GELU_C = 0.7978845608028654
GELU_K = 0.044715


def padded_2(block, sides, width):
    for axis, dim in sides:
        count = lax.axis_size(axis)
        forward = [(i, i + 1) for i in range(count - 1)]
        backward = [(target, source) for source, target in forward]
        low = lax.ppermute(
            lax.slice_in_dim(block, block.shape[dim] - width, None, axis=dim), axis, forward
        )
        high = lax.ppermute(lax.slice_in_dim(block, 0, width, axis=dim), axis, backward)
        block = jnp.concatenate([low, block, high], axis=dim)
    return block


def gelu(v):
    t = jnp.tanh(GELU_C * (v + GELU_K * v * v * v))
    return 0.5 * v * (1.0 + t)


def slope(v):
    t = jnp.tanh(GELU_C * (v + GELU_K * v * v * v))
    return 0.5 * (1.0 + t) + 0.5 * v * (1.0 - t * t) * GELU_C * (1.0 + 3.0 * GELU_K * v * v)


def stacked_taps(padded, height, width, flipped):
    pieces = []
    for row_k in range(3):
        for col_k in range(3):
            if flipped:
                pieces.append(
                    padded[:, 2 - row_k : 2 - row_k + height, 2 - col_k : 2 - col_k + width]
                )
            else:
                pieces.append(padded[:, row_k : row_k + height, col_k : col_k + width])
    return jnp.concatenate(pieces, axis=0)


def body(image, cotangent, w_reduce, w_spatial, w_expand):
    feats = image[0]
    upstream = cotangent[0]
    channels, height, width = feats.shape
    inner = w_reduce.shape[1]
    pixels = height * width * lax.axis_size("dp") * lax.axis_size("row") * lax.axis_size("col")
    scale = float(pixels) ** (-0.5)
    f32 = jnp.float32
    pre_one = jnp.einsum("chw,cm->mhw", feats, w_reduce, preferred_element_type=f32)
    hidden_one = gelu(pre_one).astype(jnp.bfloat16)
    pad_one = padded_2(hidden_one, (("row", 1), ("col", 2)), 1)
    patches = stacked_taps(pad_one, height, width, False)
    spatial_flat = w_spatial.reshape(9 * inner, inner)
    pre_two = jnp.einsum("khw,kd->dhw", patches, spatial_flat, preferred_element_type=f32)
    hidden_two = gelu(pre_two).astype(jnp.bfloat16)
    total = jnp.einsum(
        "mhw,mc->chw", hidden_two, w_expand, preferred_element_type=f32
    ) + feats.astype(f32)
    top = (upstream.astype(f32) * slope(total)).astype(jnp.bfloat16)
    grad_expand = jnp.einsum("mhw,chw->mc", hidden_two, top, preferred_element_type=f32) * scale
    back_two = (
        jnp.einsum("chw,mc->mhw", top, w_expand, preferred_element_type=f32) * slope(pre_two)
    ).astype(jnp.bfloat16)
    pad_back = padded_2(back_two, (("row", 1), ("col", 2)), 1)
    grad_spatial = (
        jnp.einsum("khw,dhw->kd", patches, back_two, preferred_element_type=f32).reshape(
            3, 3, inner, inner
        )
        * scale
    )
    back_taps = stacked_taps(pad_back, height, width, True)
    spatial_turned = jnp.transpose(w_spatial, (0, 1, 3, 2)).reshape(9 * inner, inner)
    back_pre = jnp.einsum("khw,kc->chw", back_taps, spatial_turned, preferred_element_type=f32)
    back_one = (back_pre * slope(pre_one)).astype(jnp.bfloat16)
    grad_reduce = jnp.einsum("chw,mhw->cm", feats, back_one, preferred_element_type=f32) * scale
    result = (
        jnp.einsum("mhw,cm->chw", back_one, w_reduce, preferred_element_type=f32) + top.astype(f32)
    ).astype(jnp.bfloat16)
    grad_reduce, grad_spatial, grad_expand = lax.psum(
        (grad_reduce, grad_spatial, grad_expand), ("dp", "row", "col")
    )
    return (result.reshape(1, channels, height, width), grad_reduce, grad_spatial, grad_expand)


def solution(mesh):
    in_specs = (P("dp", None, "row", "col"), P("dp", None, "row", "col"), P(), P(), P())
    out_specs = (P("dp", None, "row", "col"), P(), P(), P())
    return jax.shard_map(body, mesh=mesh, in_specs=in_specs, out_specs=out_specs, check_vma=False)
```

profile of v0, /device:TPU:8, one launch (start us, length us, event | category | flops | bytes accessed | tf_op | source)
XLA Modules:
  0.0 199.0 jit_solution(10238605451038991250)
XLA Ops:
  7.2 2.2 %copy.29 = bf16[256,24,128]{0,2,1:T(8,128)(2,1)S(1)} copy(bf16[256,24,128]{2,1,0:T(8,128)(2,1)} %bitcast.81) | data formatting | bytes 3145728 | tf_op jit(solution)/shard_map/squeeze | solution.py:47
  9.4 1.5 multiply_convert_fusion.1
  10.9 3.5 %collective-permute-start = (bf16[64,1,128]{2,0,1:T(8,128)(2,1)S(1)}, bf16[64,1,128]{2,0,1:T(8,128)(2,1)S(1)}, u32[]{:S(2)}, u32[]{:S(2)}) collective-permute-start(bf16[64,1,128]{2,0,1:T(8,128)(2,1)S(1)} %get-tuple-element.25), channel_id=1, source_target_pairs={{0,2},{2,4},{4,6},{1,3},{3,5},{5,7},{8,10},{10,12},{12,14},{9,11},... | collective-permute-start | bytes 49160 | tf_op jit(solution)/shard_map/ppermute | solution.py:15
  14.4 2.4 %collective-permute-start.1 = (bf16[64,1,128]{2,0,1:T(8,128)(2,1)S(1)}, bf16[64,1,128]{2,0,1:T(8,128)(2,1)S(1)}, u32[]{:S(2)}, u32[]{:S(2)}) collective-permute-start(bf16[64,1,128]{2,0,1:T(8,128)(2,1)S(1)} %get-tuple-element.26), channel_id=1, source_target_pairs={{2,0},{4,2},{6,4},{3,1},{5,3},{7,5},{10,8},{12,10},{14,12},{11,9},... | collective-permute-start | bytes 49160 | tf_op jit(solution)/shard_map/ppermute | solution.py:18
  16.7 3.3 %collective-permute-done.1 = bf16[64,1,128]{2,0,1:T(8,128)(2,1)S(1)} collective-permute-done((bf16[64,1,128]{2,0,1:T(8,128)(2,1)S(1)}, bf16[64,1,128]{2,0,1:T(8,128)(2,1)S(1)}, u32[]{:S(2)}, u32[]{:S(2)}) %collective-permute-start.1) | collective-permute-done | bytes 16416 | tf_op jit(solution)/shard_map/ppermute | solution.py:18
  21.1 1.3 collective-permute-start.2
  22.4 1.4 collective-permute-start.3
  23.8 2.9 %copy.19 = bf16[1,256,24,128]{1,3,2,0:T(8,128)(2,1)} copy(bf16[1,256,24,128]{3,2,1,0:T(8,128)(2,1)} %param.5) | data formatting | bytes 3145728 | tf_op args[0]
  26.7 2.8 %copy.18 = bf16[1,256,24,128]{1,3,2,0:T(8,128)(2,1)} copy(bf16[1,256,24,128]{3,2,1,0:T(8,128)(2,1)} %param.6) | data formatting | bytes 3145728 | tf_op args[1]
  33.6 2.7 %fusion.6 = bf16[256,24,128]{0,2,1:T(8,128)(2,1)S(1)} fusion(bf16[1,256,24,128]{1,3,2,0:T(8,128)(2,1)S(1)} %copy-done.4, bf16[1,256,24,128]{1,3,2,0:T(8,128)(2,1)S(1)} %copy-done.3, bf16[64,256]{1,0:T(8,128)(2,1)S(1)} %copy-done.9, f32[64,24,128]{2,0,1:T(8,128)S(1)} %convolution_bitcast_fusion.2), kind=kOutput, calls=%fused_computation.8 | convolution fusion | flops 119734272 | bytes 5537792 | tf_op jit(solution)/shard_map/mhw,mc->chw/dot_general | solution.py:61
  37.1 3.5 %collective-permute-start.4 = (bf16[64,1,128]{2,0,1:T(8,128)(2,1)S(1)}, bf16[64,1,128]{2,0,1:T(8,128)(2,1)S(1)}, u32[]{:S(2)}, u32[]{:S(2)}) collective-permute-start(bf16[64,1,128]{2,0,1:T(8,128)(2,1)S(1)} %get-tuple-element.23), channel_id=1, source_target_pairs={{0,2},{2,4},{4,6},{1,3},{3,5},{5,7},{8,10},{10,12},{12,14},{9,11},... | collective-permute-start | bytes 49160 | tf_op jit(solution)/shard_map/ppermute | solution.py:15
  40.6 2.4 %collective-permute-start.5 = (bf16[64,1,128]{2,0,1:T(8,128)(2,1)S(1)}, bf16[64,1,128]{2,0,1:T(8,128)(2,1)S(1)}, u32[]{:S(2)}, u32[]{:S(2)}) collective-permute-start(bf16[64,1,128]{2,0,1:T(8,128)(2,1)S(1)} %get-tuple-element.24), channel_id=1, source_target_pairs={{2,0},{4,2},{6,4},{3,1},{5,3},{7,5},{10,8},{12,10},{14,12},{11,9},... | collective-permute-start | bytes 49160 | tf_op jit(solution)/shard_map/ppermute | solution.py:18
  43.0 1.2 fusion.13
  44.2 2.2 %collective-permute-done.5 = bf16[64,1,128]{2,0,1:T(8,128)(2,1)S(1)} collective-permute-done((bf16[64,1,128]{2,0,1:T(8,128)(2,1)S(1)}, bf16[64,1,128]{2,0,1:T(8,128)(2,1)S(1)}, u32[]{:S(2)}, u32[]{:S(2)}) %collective-permute-start.5) | collective-permute-done | bytes 16416 | tf_op jit(solution)/shard_map/ppermute | solution.py:18
  47.3 1.3 collective-permute-start.6
  48.6 3.3 %collective-permute-start.7 = (bf16[64,26,1]{2,0,1:T(8,128)(2,1)S(1)}, bf16[64,26,1]{2,0,1:T(8,128)(2,1)S(1)}, u32[]{:S(2)}, u32[]{:S(2)}) collective-permute-start(bf16[64,26,1]{2,0,1:T(8,128)(2,1)S(1)} %get-tuple-element.17), channel_id=1, source_target_pairs={{0,1},{2,3},{4,5},{6,7},{8,9},{10,11},{12,13},{14,15},{16,17},{18,... | collective-permute-start | bytes 9992 | tf_op jit(solution)/shard_map/ppermute | solution.py:15
  51.9 1.1 fusion.14
  55.8 1.2 fusion.11
  58.0 1.6 fusion.8
  59.6 1.9 copy.28
  61.5 126.0 %all-reduce.3.cloned.1.call-done = (f32[256,64]{0,1:T(8,128)}, f32[3,3,64,64]{3,2,1,0:T(8,128)}, f32[64,256]{1,0:T(8,128)}) async-done(((f32[256,64]{0,1:T(8,128)}, f32[3,3,64,64]{3,2,1,0:T(8,128)}, f32[64,256]{1,0:T(8,128)}), (f32[256,64]{0,1:T(8,128)}, f32[3,3,64,64]{3,2,1,0:T(8,128)}, f32[64,256]{1,0:T(8,128)})) %all-reduce.3.cloned.1.call-update) | async-done | bytes 278544 | tf_op jit(solution)/shard_map/psum | solution.py:84
  187.5 1.5 copy.60
  188.9 1.7 copy.61
  190.6 1.5 copy.62
  (59 shorter events, 10.6 us)
Async XLA Ops:
  7.2 2.2 %copy-start = (bf16[256,64]{0,1:T(8,128)(2,1)S(1)}, bf16[256,64]{0,1:T(8,128)(2,1)}, u32[]{:S(2)}) copy-start(bf16[256,64]{0,1:T(8,128)(2,1)} %param.7) | copy-start | bytes 98308
  7.2 180.3 %all-reduce.3.cloned.1.call-start = ((), (), s32[]{:S(2)}) async-start(), calls=%async_computation | async-start | bytes 851968 | tf_op jit(solution)/shard_map/psum | solution.py:84
  10.9 5.8 %collective-permute-start = (bf16[64,1,128]{2,0,1:T(8,128)(2,1)S(1)}, bf16[64,1,128]{2,0,1:T(8,128)(2,1)S(1)}, u32[]{:S(2)}, u32[]{:S(2)}) collective-permute-start(bf16[64,1,128]{2,0,1:T(8,128)(2,1)S(1)} %get-tuple-element.25), channel_id=1, source_target_pairs={{0,2},{2,4},{4,6},{1,3},{3,5},{5,7},{8,10},{10,12},{12,14},{9,11},... | collective-permute-start | bytes 49160 | tf_op jit(solution)/shard_map/ppermute | solution.py:15
  14.4 5.6 %collective-permute-start.1 = (bf16[64,1,128]{2,0,1:T(8,128)(2,1)S(1)}, bf16[64,1,128]{2,0,1:T(8,128)(2,1)S(1)}, u32[]{:S(2)}, u32[]{:S(2)}) collective-permute-start(bf16[64,1,128]{2,0,1:T(8,128)(2,1)S(1)} %get-tuple-element.26), channel_id=1, source_target_pairs={{2,0},{4,2},{6,4},{3,1},{5,3},{7,5},{10,8},{12,10},{14,12},{11,9},... | collective-permute-start | bytes 49160 | tf_op jit(solution)/shard_map/ppermute | solution.py:18
  21.1 9.2 %collective-permute-start.2 = (bf16[64,26,1]{2,0,1:T(8,128)(2,1)}, bf16[64,26,1]{2,0,1:T(8,128)(2,1)S(1)}, u32[]{:S(2)}, u32[]{:S(2)}) collective-permute-start(bf16[64,26,1]{2,0,1:T(8,128)(2,1)} %get-tuple-element.22), channel_id=1, source_target_pairs={{0,1},{2,3},{4,5},{6,7},{8,9},{10,11},{12,13},{14,15},{16,17},{18,... | collective-permute-start | bytes 9992 | tf_op jit(solution)/shard_map/ppermute | solution.py:15
  22.4 7.1 %copy-start.7 = (bf16[3,3,64,64]{3,2,1,0:T(8,128)(2,1)S(1)}, bf16[3,3,64,64]{3,2,1,0:T(8,128)(2,1)}, u32[]{:S(2)}) copy-start(bf16[3,3,64,64]{3,2,1,0:T(8,128)(2,1)} %param.8) | copy-start | bytes 221188
  22.4 7.9 %collective-permute-start.3 = (bf16[64,26,1]{2,0,1:T(8,128)(2,1)S(1)}, bf16[64,26,1]{2,0,1:T(8,128)(2,1)S(1)}, u32[]{:S(2)}, u32[]{:S(2)}) collective-permute-start(bf16[64,26,1]{2,0,1:T(8,128)(2,1)S(1)} %get-tuple-element.21), channel_id=1, source_target_pairs={{1,0},{3,2},{5,4},{7,6},{9,8},{11,10},{13,12},{15,14},{17,16},{19,... | collective-permute-start | bytes 9992 | tf_op jit(solution)/shard_map/ppermute | solution.py:18
  31.7 1.4 copy-start.3
  31.7 1.9 copy-start.4
  31.8 1.9 copy-start.9
  36.4 15.5 %copy-start.1 = (bf16[256,24,128]{0,2,1:T(8,128)(2,1)}, bf16[256,24,128]{0,2,1:T(8,128)(2,1)S(1)}, u32[]{:S(2)}) copy-start(bf16[256,24,128]{0,2,1:T(8,128)(2,1)S(1)} %fusion.6) | copy-start | bytes 4718596
  37.1 7.0 %collective-permute-start.4 = (bf16[64,1,128]{2,0,1:T(8,128)(2,1)S(1)}, bf16[64,1,128]{2,0,1:T(8,128)(2,1)S(1)}, u32[]{:S(2)}, u32[]{:S(2)}) collective-permute-start(bf16[64,1,128]{2,0,1:T(8,128)(2,1)S(1)} %get-tuple-element.23), channel_id=1, source_target_pairs={{0,2},{2,4},{4,6},{1,3},{3,5},{5,7},{8,10},{10,12},{12,14},{9,11},... | collective-permute-start | bytes 49160 | tf_op jit(solution)/shard_map/ppermute | solution.py:15
  40.6 5.7 %collective-permute-start.5 = (bf16[64,1,128]{2,0,1:T(8,128)(2,1)S(1)}, bf16[64,1,128]{2,0,1:T(8,128)(2,1)S(1)}, u32[]{:S(2)}, u32[]{:S(2)}) collective-permute-start(bf16[64,1,128]{2,0,1:T(8,128)(2,1)S(1)} %get-tuple-element.24), channel_id=1, source_target_pairs={{2,0},{4,2},{6,4},{3,1},{5,3},{7,5},{10,8},{12,10},{14,12},{11,9},... | collective-permute-start | bytes 49160 | tf_op jit(solution)/shard_map/ppermute | solution.py:18
  47.3 6.5 %collective-permute-start.6 = (bf16[64,26,1]{2,0,1:T(8,128)(2,1)}, bf16[64,26,1]{2,0,1:T(8,128)(2,1)S(1)}, u32[]{:S(2)}, u32[]{:S(2)}) collective-permute-start(bf16[64,26,1]{2,0,1:T(8,128)(2,1)} %get-tuple-element.18), channel_id=1, source_target_pairs={{1,0},{3,2},{5,4},{7,6},{9,8},{11,10},{13,12},{15,14},{17,16},{19,... | collective-permute-start | bytes 9992 | tf_op jit(solution)/shard_map/ppermute | solution.py:18
  48.6 5.2 %collective-permute-start.7 = (bf16[64,26,1]{2,0,1:T(8,128)(2,1)S(1)}, bf16[64,26,1]{2,0,1:T(8,128)(2,1)S(1)}, u32[]{:S(2)}, u32[]{:S(2)}) collective-permute-start(bf16[64,26,1]{2,0,1:T(8,128)(2,1)S(1)} %get-tuple-element.17), channel_id=1, source_target_pairs={{0,1},{2,3},{4,5},{6,7},{8,9},{10,11},{12,13},{14,15},{16,17},{18,... | collective-permute-start | bytes 9992 | tf_op jit(solution)/shard_map/ppermute | solution.py:15
  54.6 1.1 copy-start.6
  54.6 1.1 copy-start.8
  55.8 2.2 %copy-start.2 = (bf16[256,24,128]{0,2,1:T(8,128)(2,1)S(1)}, bf16[256,24,128]{0,2,1:T(8,128)(2,1)}, u32[]{:S(2)}) copy-start(bf16[256,24,128]{0,2,1:T(8,128)(2,1)} %copy-done.1) | copy-start | bytes 4718596
  56.9 1.0 copy-start.5
Sparse Core Ops, SparseCore 0:
  58.1 129.3 all-reduce.2
where the time goes:
time: 199 us
  waiting for transfers between devices  131 us (66%)
  local copies, waits for them, and re-layouts  20.9 us (11%)
  starting transfers between devices  19 us (10%)
  between operations  14.4 us (7%)
  matrix products  11.8 us (6%)
    psum x1, waiting for transfers between devices, body(): lax.psum((grad_reduce, grad_spatial, grad_expand), ('dp', 'row', 'col'))  126 us
    unnamed x38, local copies, waits for them, and re-layouts  14.8 us
    ppermute x4, starting transfers between devices, padded_2(): lax.ppermute(lax.slice_in_dim(block, block.shape[dim] - width, None, axis...  11.5 us
    ppermute x4, starting transfers between devices, padded_2(): lax.ppermute(lax.slice_in_dim(block, 0, width, axis=dim), axis, backward)  7.41 us
    ppermute x4, waiting for transfers between devices, padded_2(): lax.ppermute(lax.slice_in_dim(block, 0, width, axis=dim), axis, backward)  5.42 us
  transfers between devices with their start and end apart: 9, of which 3 were waited for; matrix products, arithmetic and copies ran while one was open for 7% of the time, Pallas kernels for 0%

commit v1 on v0

--- a/solution.py
+++ b/solution.py
@@ -82,7 +82,7 @@
         jnp.einsum("mhw,cm->chw", back_one, w_reduce, preferred_element_type=f32) + top.astype(f32)
     ).astype(jnp.bfloat16)
     grad_reduce, grad_spatial, grad_expand = lax.psum(
-        (grad_reduce, grad_spatial, grad_expand), ("dp", "row", "col")
+        lax.psum((grad_reduce, grad_spatial, grad_expand), "dp"), ("row", "col")
     )
     return (result.reshape(1, channels, height, width), grad_reduce, grad_spatial, grad_expand)
 

time: 199 us -> 174 us (0.87)
  waiting for transfers between devices: 131 us -> 104 us
    psum x1 -> x2, waiting for transfers between devices: 126 us -> 98.7 us  [the longest x1 54.5 us: body(): lax.psum(lax.psum((grad_reduce, grad_spatial, grad_expand), 'dp'), ('row'...]
    unnamed x38 -> x34, local copies, waits for them, and re-layouts: 14.8 us -> 14.6 us
  transfers between devices with their start and end apart: 9 -> 10, of which waited for: 3 -> 4; matrix products, arithmetic and copies ran while one was open for 7% -> 7% of each run, Pallas kernels for 0% -> 0%
where the time goes in v1:
time: 174 us; the launch traced here: 173 us
  waiting for transfers between devices  104 us (60%)
  local copies, waits for them, and re-layouts  20.3 us (12%)
  starting transfers between devices  19.6 us (11%)
  between operations  14.4 us (8%)
  matrix products  11 us (6%)
  other arithmetic  3.41 us (2%)
    psum x1, waiting for transfers between devices, body(): lax.psum(lax.psum((grad_reduce, grad_spatial, grad_expand), 'dp'), ('row'...  54.5 us
    psum x1, waiting for transfers between devices, body(): lax.psum((grad_reduce, grad_spatial, grad_expand), 'dp')  44.1 us
    unnamed x34, local copies, waits for them, and re-layouts  14.6 us
    ppermute x4, starting transfers between devices, padded_2(): lax.ppermute(lax.slice_in_dim(block, block.shape[dim] - width, None, axis...  12.1 us
    ppermute x4, starting transfers between devices, padded_2(): lax.ppermute(lax.slice_in_dim(block, 0, width, axis=dim), axis, backward)  7.41 us
    ppermute x4, waiting for transfers between devices, padded_2(): lax.ppermute(lax.slice_in_dim(block, 0, width, axis=dim), axis, backward)  5.35 us
  transfers between devices with their start and end apart: 10, of which 4 were waited for; matrix products, arithmetic and copies ran while one was open for 7% of the time, Pallas kernels for 0%

profile of v1, /device:TPU:8, one launch (start us, length us, event | category | flops | bytes accessed | tf_op | source)
XLA Modules:
  0.0 172.8 jit_solution(4859936067596511971)
XLA Ops:
  7.2 2.1 %copy.29 = bf16[256,24,128]{0,2,1:T(8,128)(2,1)S(1)} copy(bf16[256,24,128]{2,1,0:T(8,128)(2,1)} %bitcast.81) | data formatting | bytes 3145728 | tf_op jit(solution)/shard_map/squeeze | solution.py:47
  10.0 3.5 %collective-permute-start = (bf16[64,1,128]{2,0,1:T(8,128)(2,1)S(1)}, bf16[64,1,128]{2,0,1:T(8,128)(2,1)S(1)}, u32[]{:S(2)}, u32[]{:S(2)}) collective-permute-start(bf16[64,1,128]{2,0,1:T(8,128)(2,1)S(1)} %get-tuple-element.28), channel_id=1, source_target_pairs={{0,2},{2,4},{4,6},{1,3},{3,5},{5,7},{8,10},{10,12},{12,14},{9,11},... | collective-permute-start | bytes 49160 | tf_op jit(solution)/shard_map/ppermute | solution.py:15
  13.5 2.4 %collective-permute-start.1 = (bf16[64,1,128]{2,0,1:T(8,128)(2,1)S(1)}, bf16[64,1,128]{2,0,1:T(8,128)(2,1)S(1)}, u32[]{:S(2)}, u32[]{:S(2)}) collective-permute-start(bf16[64,1,128]{2,0,1:T(8,128)(2,1)S(1)} %get-tuple-element.29), channel_id=1, source_target_pairs={{2,0},{4,2},{6,4},{3,1},{5,3},{7,5},{10,8},{12,10},{14,12},{11,9},... | collective-permute-start | bytes 49160 | tf_op jit(solution)/shard_map/ppermute | solution.py:18
  15.9 3.3 %collective-permute-done.1 = bf16[64,1,128]{2,0,1:T(8,128)(2,1)S(1)} collective-permute-done((bf16[64,1,128]{2,0,1:T(8,128)(2,1)S(1)}, bf16[64,1,128]{2,0,1:T(8,128)(2,1)S(1)}, u32[]{:S(2)}, u32[]{:S(2)}) %collective-permute-start.1) | collective-permute-done | bytes 16416 | tf_op jit(solution)/shard_map/ppermute | solution.py:18
  20.3 1.3 collective-permute-start.2
  21.7 1.4 collective-permute-start.3
  23.1 2.9 %copy.19 = bf16[1,256,24,128]{1,3,2,0:T(8,128)(2,1)} copy(bf16[1,256,24,128]{3,2,1,0:T(8,128)(2,1)} %param.5) | data formatting | bytes 3145728 | tf_op args[0]
  26.0 2.8 %copy.18 = bf16[1,256,24,128]{1,3,2,0:T(8,128)(2,1)} copy(bf16[1,256,24,128]{3,2,1,0:T(8,128)(2,1)} %param.6) | data formatting | bytes 3145728 | tf_op args[1]
  28.9 1.5 pad_maximum_fusion
  33.2 2.7 %fusion.6 = bf16[256,24,128]{0,2,1:T(8,128)(2,1)S(1)} fusion(bf16[1,256,24,128]{1,3,2,0:T(8,128)(2,1)S(1)} %copy-done.4, bf16[1,256,24,128]{1,3,2,0:T(8,128)(2,1)S(1)} %copy-done.3, bf16[64,256]{1,0:T(8,128)(2,1)S(1)} %copy-done.7, f32[64,24,128]{2,0,1:T(8,128)S(1)} %convolution_bitcast_fusion.2), kind=kOutput, calls=%fused_computation.8 | convolution fusion | flops 119734272 | bytes 5537792 | tf_op jit(solution)/shard_map/mhw,mc->chw/dot_general | solution.py:61
  36.7 3.5 %collective-permute-start.4 = (bf16[64,1,128]{2,0,1:T(8,128)(2,1)S(1)}, bf16[64,1,128]{2,0,1:T(8,128)(2,1)S(1)}, u32[]{:S(2)}, u32[]{:S(2)}) collective-permute-start(bf16[64,1,128]{2,0,1:T(8,128)(2,1)S(1)} %get-tuple-element.26), channel_id=1, source_target_pairs={{0,2},{2,4},{4,6},{1,3},{3,5},{5,7},{8,10},{10,12},{12,14},{9,11},... | collective-permute-start | bytes 49160 | tf_op jit(solution)/shard_map/ppermute | solution.py:15
  40.2 2.4 %collective-permute-start.5 = (bf16[64,1,128]{2,0,1:T(8,128)(2,1)S(1)}, bf16[64,1,128]{2,0,1:T(8,128)(2,1)S(1)}, u32[]{:S(2)}, u32[]{:S(2)}) collective-permute-start(bf16[64,1,128]{2,0,1:T(8,128)(2,1)S(1)} %get-tuple-element.27), channel_id=1, source_target_pairs={{2,0},{4,2},{6,4},{3,1},{5,3},{7,5},{10,8},{12,10},{14,12},{11,9},... | collective-permute-start | bytes 49160 | tf_op jit(solution)/shard_map/ppermute | solution.py:18
  42.6 1.2 fusion.13
  43.8 2.1 %collective-permute-done.5 = bf16[64,1,128]{2,0,1:T(8,128)(2,1)S(1)} collective-permute-done((bf16[64,1,128]{2,0,1:T(8,128)(2,1)S(1)}, bf16[64,1,128]{2,0,1:T(8,128)(2,1)S(1)}, u32[]{:S(2)}, u32[]{:S(2)}) %collective-permute-start.5) | collective-permute-done | bytes 16416 | tf_op jit(solution)/shard_map/ppermute | solution.py:18
  47.0 1.3 collective-permute-start.6
  48.3 3.8 %collective-permute-start.7 = (bf16[64,26,1]{2,0,1:T(8,128)(2,1)}, bf16[64,26,1]{2,0,1:T(8,128)(2,1)}, u32[]{:S(2)}, u32[]{:S(2)}) collective-permute-start(bf16[64,26,1]{2,0,1:T(8,128)(2,1)} %get-tuple-element.20), channel_id=1, source_target_pairs={{0,1},{2,3},{4,5},{6,7},{8,9},{10,11},{12,13},{14,15},{16,17},{18,... | collective-permute-start | bytes 9992 | tf_op jit(solution)/shard_map/ppermute | solution.py:15
  54.1 1.5 maximum_maximum_fusion.1
  59.1 44.1 %all-reduce.7.cloned.1.call-done = (f32[256,64]{0,1:T(8,128)}, f32[3,3,64,64]{3,2,1,0:T(8,128)}, f32[64,256]{1,0:T(8,128)}) async-done(((f32[256,64]{0,1:T(8,128)}, f32[3,3,64,64]{3,2,1,0:T(8,128)}, f32[64,256]{1,0:T(8,128)}), (f32[256,64]{0,1:T(8,128)}, f32[3,3,64,64]{3,2,1,0:T(8,128)}, f32[64,256]{1,0:T(8,128)})) %all-reduce.7.cloned.1.call-update) | async-done | bytes 278544 | tf_op jit(solution)/shard_map/psum | solution.py:85
  103.2 1.6 fusion.8
  104.8 1.9 %copy.28 = bf16[1,256,24,128]{3,2,1,0:T(8,128)(2,1)} copy(bf16[1,256,24,128]{1,3,2,0:T(8,128)(2,1)S(1)} %fusion.8) | data formatting | bytes 3145728
  106.7 54.5 %all-reduce.5.cloned.1.call-done = (f32[256,64]{0,1:T(8,128)}, f32[3,3,64,64]{3,2,1,0:T(8,128)}, f32[64,256]{1,0:T(8,128)}) async-done(((f32[256,64]{0,1:T(8,128)}, f32[3,3,64,64]{3,2,1,0:T(8,128)}, f32[64,256]{1,0:T(8,128)}), (f32[256,64]{0,1:T(8,128)}, f32[3,3,64,64]{3,2,1,0:T(8,128)}, f32[64,256]{1,0:T(8,128)})) %all-reduce.5.cloned.1.call-update) | async-done | bytes 278544 | tf_op jit(solution)/shard_map/psum | solution.py:84
  161.3 1.5 copy.63
  162.8 1.7 copy.64
  164.5 1.5 copy.65
  (58 shorter events, 11.8 us)
Async XLA Ops:
  7.2 2.2 %copy-start = (bf16[256,64]{0,1:T(8,128)(2,1)S(1)}, bf16[256,64]{0,1:T(8,128)(2,1)}, u32[]{:S(2)}) copy-start(bf16[256,64]{0,1:T(8,128)(2,1)} %param.7) | copy-start | bytes 98308
  7.2 96.0 %all-reduce.7.cloned.1.call-start = ((), (), s32[]{:S(2)}) async-start(), calls=%async_computation.1 | async-start | bytes 851968 | tf_op jit(solution)/shard_map/psum | solution.py:85
  10.0 5.9 %collective-permute-start = (bf16[64,1,128]{2,0,1:T(8,128)(2,1)S(1)}, bf16[64,1,128]{2,0,1:T(8,128)(2,1)S(1)}, u32[]{:S(2)}, u32[]{:S(2)}) collective-permute-start(bf16[64,1,128]{2,0,1:T(8,128)(2,1)S(1)} %get-tuple-element.28), channel_id=1, source_target_pairs={{0,2},{2,4},{4,6},{1,3},{3,5},{5,7},{8,10},{10,12},{12,14},{9,11},... | collective-permute-start | bytes 49160 | tf_op jit(solution)/shard_map/ppermute | solution.py:15
  13.5 5.6 %collective-permute-start.1 = (bf16[64,1,128]{2,0,1:T(8,128)(2,1)S(1)}, bf16[64,1,128]{2,0,1:T(8,128)(2,1)S(1)}, u32[]{:S(2)}, u32[]{:S(2)}) collective-permute-start(bf16[64,1,128]{2,0,1:T(8,128)(2,1)S(1)} %get-tuple-element.29), channel_id=1, source_target_pairs={{2,0},{4,2},{6,4},{3,1},{5,3},{7,5},{10,8},{12,10},{14,12},{11,9},... | collective-permute-start | bytes 49160 | tf_op jit(solution)/shard_map/ppermute | solution.py:18
  20.3 8.6 %collective-permute-start.2 = (bf16[64,26,1]{2,0,1:T(8,128)(2,1)}, bf16[64,26,1]{2,0,1:T(8,128)(2,1)S(1)}, u32[]{:S(2)}, u32[]{:S(2)}) collective-permute-start(bf16[64,26,1]{2,0,1:T(8,128)(2,1)} %get-tuple-element.25), channel_id=1, source_target_pairs={{0,1},{2,3},{4,5},{6,7},{8,9},{10,11},{12,13},{14,15},{16,17},{18,... | collective-permute-start | bytes 9992 | tf_op jit(solution)/shard_map/ppermute | solution.py:15
  21.6 7.1 %copy-start.6 = (bf16[3,3,64,64]{3,2,1,0:T(8,128)(2,1)S(1)}, bf16[3,3,64,64]{3,2,1,0:T(8,128)(2,1)}, u32[]{:S(2)}) copy-start(bf16[3,3,64,64]{3,2,1,0:T(8,128)(2,1)} %param.8) | copy-start | bytes 221188
  21.7 7.3 %collective-permute-start.3 = (bf16[64,26,1]{2,0,1:T(8,128)(2,1)}, bf16[64,26,1]{2,0,1:T(8,128)(2,1)}, u32[]{:S(2)}, u32[]{:S(2)}) collective-permute-start(bf16[64,26,1]{2,0,1:T(8,128)(2,1)} %get-tuple-element.24), channel_id=1, source_target_pairs={{1,0},{3,2},{5,4},{7,6},{9,8},{11,10},{13,12},{15,14},{17,16},{19,... | collective-permute-start | bytes 9992 | tf_op jit(solution)/shard_map/ppermute | solution.py:18
  31.3 1.4 copy-start.3
  31.4 1.9 %copy-start.4 = (bf16[1,256,24,128]{1,3,2,0:T(8,128)(2,1)S(1)}, bf16[1,256,24,128]{1,3,2,0:T(8,128)(2,1)}, u32[]{:S(2)}) copy-start(bf16[1,256,24,128]{1,3,2,0:T(8,128)(2,1)} %copy.18) | copy-start | bytes 4718596
  31.4 1.9 %copy-start.7 = (bf16[64,256]{1,0:T(8,128)(2,1)S(1)}, bf16[64,256]{1,0:T(8,128)(2,1)}, u32[]{:S(2)}) copy-start(bf16[64,256]{1,0:T(8,128)(2,1)} %param.9) | copy-start | bytes 98308
  36.0 16.2 %copy-start.1 = (bf16[256,24,128]{0,2,1:T(8,128)(2,1)}, bf16[256,24,128]{0,2,1:T(8,128)(2,1)S(1)}, u32[]{:S(2)}) copy-start(bf16[256,24,128]{0,2,1:T(8,128)(2,1)S(1)} %fusion.6) | copy-start | bytes 4718596
  36.7 7.0 %collective-permute-start.4 = (bf16[64,1,128]{2,0,1:T(8,128)(2,1)S(1)}, bf16[64,1,128]{2,0,1:T(8,128)(2,1)S(1)}, u32[]{:S(2)}, u32[]{:S(2)}) collective-permute-start(bf16[64,1,128]{2,0,1:T(8,128)(2,1)S(1)} %get-tuple-element.26), channel_id=1, source_target_pairs={{0,2},{2,4},{4,6},{1,3},{3,5},{5,7},{8,10},{10,12},{12,14},{9,11},... | collective-permute-start | bytes 49160 | tf_op jit(solution)/shard_map/ppermute | solution.py:15
  40.2 5.6 %collective-permute-start.5 = (bf16[64,1,128]{2,0,1:T(8,128)(2,1)S(1)}, bf16[64,1,128]{2,0,1:T(8,128)(2,1)S(1)}, u32[]{:S(2)}, u32[]{:S(2)}) collective-permute-start(bf16[64,1,128]{2,0,1:T(8,128)(2,1)S(1)} %get-tuple-element.27), channel_id=1, source_target_pairs={{2,0},{4,2},{6,4},{3,1},{5,3},{7,5},{10,8},{12,10},{14,12},{11,9},... | collective-permute-start | bytes 49160 | tf_op jit(solution)/shard_map/ppermute | solution.py:18
  47.0 7.1 %collective-permute-start.6 = (bf16[64,26,1]{2,0,1:T(8,128)(2,1)}, bf16[64,26,1]{2,0,1:T(8,128)(2,1)S(1)}, u32[]{:S(2)}, u32[]{:S(2)}) collective-permute-start(bf16[64,26,1]{2,0,1:T(8,128)(2,1)} %get-tuple-element.21), channel_id=1, source_target_pairs={{1,0},{3,2},{5,4},{7,6},{9,8},{11,10},{13,12},{15,14},{17,16},{19,... | collective-permute-start | bytes 9992 | tf_op jit(solution)/shard_map/ppermute | solution.py:18
  48.3 5.8 %collective-permute-start.7 = (bf16[64,26,1]{2,0,1:T(8,128)(2,1)}, bf16[64,26,1]{2,0,1:T(8,128)(2,1)}, u32[]{:S(2)}, u32[]{:S(2)}) collective-permute-start(bf16[64,26,1]{2,0,1:T(8,128)(2,1)} %get-tuple-element.20), channel_id=1, source_target_pairs={{0,1},{2,3},{4,5},{6,7},{8,9},{10,11},{12,13},{14,15},{16,17},{18,... | collective-permute-start | bytes 9992 | tf_op jit(solution)/shard_map/ppermute | solution.py:15
  57.9 1.1 copy-start.5
  57.9 45.3 %copy-start.2 = (bf16[256,24,128]{0,2,1:T(8,128)(2,1)S(1)}, bf16[256,24,128]{0,2,1:T(8,128)(2,1)}, u32[]{:S(2)}) copy-start(bf16[256,24,128]{0,2,1:T(8,128)(2,1)} %copy-done.1) | copy-start | bytes 4718596
  59.0 102.3 %all-reduce.5.cloned.1.call-start = ((), (), s32[]{:S(2)}) async-start(), calls=%async_computation | async-start | bytes 851968 | tf_op jit(solution)/shard_map/psum | solution.py:84
Sparse Core Ops, SparseCore 0:
  59.1 44.0 all-reduce.6
  105.7 55.5 all-reduce.4
